TPU v7x, 32 devices: a whole 2x2x4 slice. The times are simulated.
32 devices in a mesh: mem: 16 (over z, y, x), row: 2 (over core).
Axes of the slice: x: 2, y: 2, z: 4, core: 2. Of those that a mesh axis runs over, the one named last changes fastest.
Arguments:
- realization_stack: float32 [16, 5, 32, 256], P('mem', None, 'row'), may hold values from -6 to 6
- velocity: float32 [2, 32, 256], P(None, 'row'), may hold values from -0.25 to 0.25
- diffusion: float32 [5], replicated, may hold values from 0.04 to 0.12
- obs_cell: int32 [2048], replicated, may hold values from 0 to 40959
- obs_order: int32 [2048], replicated, may hold values from 0 to 2047, each once
- obs_value: float32 [2048], replicated, may hold values from -6 to 6
- obs_var: float32 [2048], replicated, may hold values from 0.2 to 2
- field_mask: int32 [5, 5], replicated, may hold values 0 or 1
Outputs:
- analysis: float32 [16, 5, 2, 16, 256], P(None, None, 'row', 'mem')
Inputs may be any that keep to these rules, and one draw needn't show every extreme that they name: `obs_cell`: a flat index field * 32 * 256 + row * 256 + column. `obs_order`: each of 0 to 2047 exactly once.
All inputs are finite; a program needn't handle non-finite values.
Results may differ from a plain program's by a relative error of at most 0.0003.
Values sent between devices are 32-bit elements; how exact they have to be, the bound alone decides.
No kernel may reach another device: no remote copies, remote signals or barrier semaphores. Data moves between devices by JAX's collectives and lax.ppermute only.
A program may use at most 64 MiB of HBM per device.

v0:
```python
import jax
import jax.numpy as jnp
from jax import lax
from jax.sharding import PartitionSpec as P

SUBSTEPS = 4
BATCHES = 2
LOC_HALF = 32
precise = lax.Precision.HIGHEST


def extended(shard, sides, width):
    for axis, dim in sides:
        count, length = (lax.axis_size(axis), shard.shape[dim])
        up = [(i, (i + 1) % count) for i in range(count - 1)]
        down = [(j, i) for i, j in up]
        last = lax.slice_in_dim(shard, length - width, length, axis=dim)
        initial = lax.slice_in_dim(shard, 0, width, axis=dim)
        before = lax.ppermute(last, axis, up)
        after = lax.ppermute(initial, axis, down)
        shard = jnp.concatenate([before, shard, after], axis=dim)
    return shard


def advance(padded, velocity, diffusion):
    spec_pad = ((0, 0),) * (padded.ndim - 1) + ((1, 1),)
    col_padded = jnp.pad(padded, spec_pad)
    centre = col_padded[..., 1:-1, 1:-1]
    north_cell = col_padded[..., :-2, 1:-1]
    south_cell = col_padded[..., 2:, 1:-1]
    west_cell = col_padded[..., 1:-1, :-2]
    east_cell = col_padded[..., 1:-1, 2:]
    along_col = velocity[0]
    along_row = velocity[1]
    spread = north_cell + south_cell + west_cell + east_cell - 4.0 * centre
    carried = (
        jnp.maximum(along_col, 0.0) * (centre - west_cell)
        + jnp.minimum(along_col, 0.0) * (east_cell - centre)
        + jnp.maximum(along_row, 0.0) * (centre - north_cell)
        + jnp.minimum(along_row, 0.0) * (south_cell - centre)
    )
    return centre + diffusion[:, None, None] * spread - carried


def gaspari(dist_sq):
    scaled = jnp.sqrt(dist_sq) / LOC_HALF
    clipped = jnp.maximum(scaled, 1.0)
    inner_part = (
        ((-0.25 * scaled + 0.5) * scaled + 0.625) * scaled - 5.0 / 3.0
    ) * scaled * scaled + 1.0
    outer_part = (
        ((((scaled / 12.0 - 0.5) * scaled + 0.625) * scaled + 5.0 / 3.0) * scaled - 5.0) * scaled
        + 4.0
        - 2.0 / (3.0 * clipped)
    )
    return jnp.where(scaled <= 1.0, inner_part, jnp.where(scaled <= 2.0, outer_part, 0.0))


def decode(flat_cells, total_rows, n_cols):
    field_ids = flat_cells // (total_rows * n_cols)
    row_ids = flat_cells // n_cols % total_rows
    col_ids = flat_cells % n_cols
    return (field_ids, row_ids, col_ids)


def innovations(priors, obs_values, obs_noise):
    members = priors.shape[0]
    average = jnp.mean(priors, axis=0)
    anomaly = priors - average
    spread = jnp.sum(anomaly * anomaly, axis=0) / (members - 1)
    variance_sum = spread + obs_noise
    root_sum = jnp.sqrt(variance_sum)
    shrink = 1.0 / (root_sum * (jnp.sqrt(obs_noise) + root_sum))
    adjust = (obs_values - average) / variance_sum - shrink * anomaly
    return (anomaly, adjust)


def regress(
    ensemble_now, base_row, obs_field, obs_row, obs_col, anomaly, adjust, field_mask, n_cols
):
    members, n_cells = ensemble_now.shape
    n_fields = field_mask.shape[0]
    per_field = n_cells // n_fields
    local_ids = lax.iota(jnp.int32, per_field)
    cell_row = (base_row + local_ids // n_cols).astype(jnp.float32)
    cell_col = (local_ids % n_cols).astype(jnp.float32)
    centred = ensemble_now - jnp.mean(ensemble_now, axis=0)
    mask_float = field_mask.astype(jnp.float32)
    total_obs = obs_field.shape[0]
    obs_block = min(256, total_obs)
    increment = jnp.zeros_like(ensemble_now)
    for offset in range(0, total_obs, obs_block):
        row_gap = cell_row[:, None] - obs_row[None, offset : offset + obs_block].astype(jnp.float32)
        col_gap = cell_col[:, None] - obs_col[None, offset : offset + obs_block].astype(jnp.float32)
        closeness = gaspari(row_gap * row_gap + col_gap * col_gap)
        field_hot = (
            obs_field[None, offset : offset + obs_block] == lax.iota(jnp.int32, n_fields)[:, None]
        ).astype(jnp.float32)
        allowed = jnp.dot(mask_float, field_hot, precision=precise)
        covariance = lax.dot_general(
            centred,
            anomaly[:, offset : offset + obs_block],
            (((0,), (0,)), ((), ())),
            precision=precise,
        )
        weights = (
            covariance.reshape(n_fields, per_field, obs_block)
            * (closeness[None] * allowed[:, None, :])
            / (members - 1)
        )
        increment = increment + lax.dot_general(
            adjust[:, offset : offset + obs_block],
            weights.reshape(n_cells, obs_block),
            (((1,), (1,)), ((), ())),
            precision=precise,
        )
    return ensemble_now + increment


def per_device(
    realization_stack, velocity, diffusion, obs_cell, obs_order, obs_value, obs_var, field_mask
):
    local_members = realization_stack.shape[0]
    n_fields = realization_stack.shape[1]
    rows_here = realization_stack.shape[2]
    n_cols = realization_stack.shape[3]
    n_mem = lax.axis_size("mem")
    n_slab = lax.axis_size("row")
    total_members = local_members * n_mem
    total_rows = rows_here * n_slab
    slab_index = lax.axis_index("row")
    member_index = lax.axis_index("mem")
    row_sub = rows_here // n_mem
    current = realization_stack
    for substep in range(SUBSTEPS):
        padded = extended(current, (("row", 2),), 1)
        current = advance(padded, velocity, diffusion)
    field_all, row_all, col_all = decode(obs_cell, total_rows, n_cols)
    batch_size = obs_cell.shape[0] // BATCHES
    layout = lax.all_to_all(current, "mem", split_axis=2, concat_axis=0, tiled=True)
    ensemble_now = layout.reshape(total_members, -1)
    base_row = slab_index * rows_here + member_index * row_sub
    for batch_num in range(BATCHES):
        picked = obs_order[batch_num * batch_size : (batch_num + 1) * batch_size]
        obs_field = field_all[picked]
        obs_row = row_all[picked]
        obs_col = col_all[picked]
        owned = ((obs_row >= base_row) & (obs_row < base_row + row_sub)).astype(jnp.float32)
        local_ids = (
            obs_field * row_sub * n_cols
            + jnp.clip(obs_row - base_row, 0, row_sub - 1) * n_cols
            + obs_col
        )
        partial_priors = jnp.take(ensemble_now, local_ids, axis=1) * owned[None, :]
        priors = lax.psum(partial_priors, ("mem", "row"))
        anomaly, adjust = innovations(priors, obs_value[picked], obs_var[picked])
        ensemble_now = regress(
            ensemble_now, base_row, obs_field, obs_row, obs_col, anomaly, adjust, field_mask, n_cols
        )
    return ensemble_now.reshape(total_members, n_fields, 1, row_sub, n_cols)


def solution(mesh):
    in_specs = (P("mem", None, "row", None), P(None, "row", None), P(), P(), P(), P(), P(), P())
    out_specs = P(None, None, "row", "mem", None)
    return jax.shard_map(
        per_device, mesh=mesh, in_specs=in_specs, out_specs=out_specs, check_vma=False
    )
```

profile of v0, /device:TPU:0, one launch (start us, length us, event | category | flops | bytes accessed | tf_op | source)
XLA Modules:
  0.0 403.0 jit_solution(6026265140585205028)
XLA Ops:
  6.5 1.0 copy.33
  7.5 1.3 collective-permute-start.1
  8.8 3.0 collective-permute-start
  11.9 0.7 add_select_fusion.1
  12.6 0.7 fusion.124
  13.3 6.1 %gather_fusion.8 = s32[1024]{0:T(1024)S(1)} fusion(s32[2048]{0:T(1024)S(1)} %get-tuple-element.33, s32[1024]{0:T(1024)S(1)} %get-tuple-element.28), kind=kCustom, calls=%fused_computation.10 | custom fusion | bytes 12288 | tf_op jit(solution)/shard_map/gather | solution.py:147
  19.4 6.2 %gather_fusion.7 = s32[1024]{0:T(1024)S(1)} fusion(s32[2048]{0:T(1024)S(1)} %get-tuple-element.32, s32[1024]{0:T(1024)S(1)} %get-tuple-element.28), kind=kCustom, calls=%fused_computation.9 | custom fusion | bytes 12288 | tf_op jit(solution)/shard_map/gather | solution.py:146
  25.6 6.2 %gather_fusion.3 = s32[1024]{0:T(1024)S(1)} fusion(s32[2048]{0:T(1024)S(1)} %get-tuple-element.33, s32[1024]{0:T(1024)S(1)} %get-tuple-element.29), kind=kCustom, calls=%fused_computation.5 | custom fusion | bytes 12288 | tf_op jit(solution)/shard_map/gather | solution.py:147
  31.8 6.2 %gather_fusion.2 = s32[1024]{0:T(1024)S(1)} fusion(s32[2048]{0:T(1024)S(1)} %get-tuple-element.32, s32[1024]{0:T(1024)S(1)} %get-tuple-element.29), kind=kCustom, calls=%fused_computation.4 | custom fusion | bytes 12288 | tf_op jit(solution)/shard_map/gather | solution.py:146
  37.9 6.2 %gather_fusion.1 = s32[1024]{0:T(1024)S(1)} fusion(s32[2048]{0:T(1024)S(1)} %get-tuple-element.34, s32[1024]{0:T(1024)S(1)} %get-tuple-element.29), kind=kCustom, calls=%fused_computation.3 | custom fusion | bytes 12288 | tf_op jit(solution)/shard_map/gather | solution.py:145
  44.1 6.2 %gather_fusion.6 = s32[1024]{0:T(1024)S(1)} fusion(s32[2048]{0:T(1024)S(1)} %get-tuple-element.34, s32[1024]{0:T(1024)S(1)} %get-tuple-element.28), kind=kCustom, calls=%fused_computation.8 | custom fusion | bytes 12288 | tf_op jit(solution)/shard_map/gather | solution.py:145
  51.1 3.7 fusion.25
  54.8 0.2 broadcast_multiply_fusion.2
  55.0 1.7 broadcast_multiply_fusion
  57.0 0.1 fusion.87
  57.2 1.3 collective-permute-start.3
  58.5 3.0 collective-permute-start.2
  61.6 0.7 collective-permute-done.2
  62.4 0.1 fusion.74
  62.6 1.3 collective-permute-start.5
  63.9 3.0 collective-permute-start.4
  67.1 0.7 collective-permute-done.4
  67.9 0.1 fusion.61
  68.0 1.3 collective-permute-start.7
  69.3 3.0 collective-permute-start.6
  72.4 6.2 %gather_fusion = f32[1024]{0:T(1024)S(1)} fusion(f32[2048]{0:T(1024)S(1)} %copy-done, s32[1024]{0:T(1024)S(1)} %get-tuple-element.29), kind=kCustom, calls=%fused_computation.2 | custom fusion | bytes 12288 | tf_op jit(solution)/shard_map/gather | solution.py:156
  78.6 6.2 %gather_fusion.5 = f32[1024]{0:T(1024)S(1)} fusion(f32[2048]{0:T(1024)S(1)} %copy-done, s32[1024]{0:T(1024)S(1)} %get-tuple-element.28), kind=kCustom, calls=%fused_computation.7 | custom fusion | bytes 12288 | tf_op jit(solution)/shard_map/gather | solution.py:156
  84.7 6.2 %gather_fusion.4 = f32[1024]{0:T(1024)S(1)} fusion(f32[2048]{0:T(1024)S(1)} %copy-done.1, s32[1024]{0:T(1024)S(1)} %get-tuple-element.29), kind=kCustom, calls=%fused_computation.6 | custom fusion | bytes 12288 | tf_op jit(solution)/shard_map/gather | solution.py:156
  90.9 6.2 %gather_fusion.9 = f32[1024]{0:T(1024)S(1)} fusion(f32[2048]{0:T(1024)S(1)} %copy-done.1, s32[1024]{0:T(1024)S(1)} %get-tuple-element.28), kind=kCustom, calls=%fused_computation.11 | custom fusion | bytes 12288 | tf_op jit(solution)/shard_map/gather | solution.py:156
  97.2 0.8 fusion.48
  98.0 8.3 %all-to-all-start = ((f32[1,5,16,256]{3,1,0,2:T(8,128)}), f32[1,5,16,256]{3,1,0,2:T(8,128)S(1)}, u32[]{:S(2)}, u32[]{:S(2)}) async-start(f32[1,5,16,256]{3,1,0,2:T(8,128)} %fusion.48), calls=%async_computation | async-start | bytes 262144 | tf_op jit(solution)/shard_map/all_to_all | solution.py:140
  106.4 7.7 %all-to-all-done = f32[1,5,16,256]{3,1,0,2:T(8,128)S(1)} async-done(((f32[1,5,16,256]{3,1,0,2:T(8,128)}), f32[1,5,16,256]{3,1,0,2:T(8,128)S(1)}, u32[]{:S(2)}, u32[]{:S(2)}) %all-to-all-start) | async-done | bytes 81952 | tf_op jit(solution)/shard_map/all_to_all | solution.py:140
  114.2 0.2 copy.38
  114.4 4.0 gather_fusion.10
  118.4 1.2 copy.39
  119.7 0.7 bitcast_multiply_fusion.1
  120.3 0.2 all-reduce.9.cloned.1.call-start
  120.6 114.6 %all-reduce.7.cloned.1.call-done = f32[16,1024]{1,0:T(8,128)} async-done(((f32[16,1024]{1,0:T(8,128)}), f32[16,1024]{1,0:T(8,128)}) %all-reduce.7.cloned.1.call-update) | async-done | bytes 65552 | tf_op jit(solution)/shard_map/psum | solution.py:155
  235.2 0.9 reduce_sum.54
  236.0 0.9 multiply_reduce_fusion.1
  237.0 1.3 fusion.9
  238.2 1.2 fusion.115
  239.4 1.2 fusion.8
  240.7 1.2 convolution_add_fusion.5
  241.9 1.2 fusion.7
  243.2 1.2 convolution_add_fusion.4
  244.4 1.2 fusion.6
  245.6 1.2 fusion.152
  246.8 0.2 copy.44
  247.1 4.2 %gather_fusion.11 = f32[1024,16]{1,0:T(8,128)} fusion(f32[16,1280]{0,1:T(8,128)S(1)} %copy.44, s32[1024]{0:T(1024)S(1)} %broadcast_clamp_fusion), kind=kCustom, calls=%fused_computation.1.clone | custom fusion | bytes 135168 | tf_op jit(solution)/shard_map/jit(_take)/gather | solution.py:154
  251.3 2.2 bitcast_multiply_fusion
  253.5 128.8 %all-reduce.9.cloned.1.call-done = f32[16,1024]{0,1:T(8,128)} async-done(((f32[16,1024]{0,1:T(8,128)}), f32[16,1024]{0,1:T(8,128)}) %all-reduce.9.cloned.1.call-update) | async-done | bytes 65552 | tf_op jit(solution)/shard_map/psum | solution.py:155
  382.3 1.2 reduce_sum.57
  383.5 1.4 multiply_reduce_fusion
  384.9 1.3 fusion
  386.2 1.2 fusion.1
  387.5 1.2 fusion.2
  388.8 1.2 fusion.3
  390.1 0.3 multiply_subtract_fusion
  390.4 1.2 fusion.42
  391.7 1.3 convolution_add_fusion.2
  392.9 1.3 convolution_add_fusion.1
  394.2 1.3 fusion.4
  395.5 0.7 reshape.1048
  (70 shorter events, 2.0 us)
Async XLA Ops:
  6.5 65.8 %copy-start = (f32[2048]{0:T(1024)S(1)}, f32[2048]{0:T(1024)}, u32[]{:S(2)}) copy-start(f32[2048]{0:T(1024)} %param.15) | copy-start | bytes 24580
  7.5 49.4 %collective-permute-start.1 = (f32[1,5,1,256]{3,1,0,2:T(8,128)S(1)}, f32[1,5,1,256]{3,1,0,2:T(8,128)S(1)}, u32[]{:S(2)}, u32[]{:S(2)}) collective-permute-start(f32[1,5,1,256]{3,1,0,2:T(8,128)S(1)} %get-tuple-element.21), channel_id=1, source_target_pairs={{1,0},{3,2},{5,4},{7,6},{9,8},{11,10},{13,12},{15,14},{17,16},{19,... | collective-permute-start | bytes 15368 | tf_op jit(solution)/shard_map/ppermute | solution.py:20
  8.8 48.1 %collective-permute-start = (f32[1,5,1,256]{3,1,0,2:T(8,128)S(1)}, f32[1,5,1,256]{3,1,0,2:T(8,128)S(1)}, u32[]{:S(2)}, u32[]{:S(2)}) collective-permute-start(f32[1,5,1,256]{3,1,0,2:T(8,128)S(1)} %get-tuple-element.20), channel_id=1, source_target_pairs={{0,1},{2,3},{4,5},{6,7},{8,9},{10,11},{12,13},{14,15},{16,17},{18,... | collective-permute-start | bytes 15368 | tf_op jit(solution)/shard_map/ppermute | solution.py:19
  44.1 6.2 %copy-start.9 = (f32[2,16,256]{2,1,0:T(8,128)S(1)}, f32[2,16,256]{2,1,0:T(8,128)}, u32[]{:S(2)}) copy-start(f32[2,16,256]{2,1,0:T(8,128)} %param.11) | copy-start | bytes 98308
  44.1 6.3 %copy-start.8 = (s32[5,5]{1,0:T(8,128)S(1)}, s32[5,5]{1,0:T(8,128)}, u32[]{:S(2)}) copy-start(s32[5,5]{1,0:T(8,128)} %param.17) | copy-start | bytes 304
  55.0 2.0 copy-start.10
  57.2 4.5 %collective-permute-start.3 = (f32[1,5,1,256]{3,1,0,2:T(8,128)S(1)}, f32[1,5,1,256]{3,1,0,2:T(8,128)S(1)}, u32[]{:S(2)}, u32[]{:S(2)}) collective-permute-start(f32[1,5,1,256]{3,1,0,2:T(8,128)S(1)} %get-tuple-element.19), channel_id=1, source_target_pairs={{1,0},{3,2},{5,4},{7,6},{9,8},{11,10},{13,12},{15,14},{17,16},{19,... | collective-permute-start | bytes 15368 | tf_op jit(solution)/shard_map/ppermute | solution.py:20
  58.5 3.8 collective-permute-start.2
  62.6 4.5 %collective-permute-start.5 = (f32[1,5,1,256]{3,1,0,2:T(8,128)S(1)}, f32[1,5,1,256]{3,1,0,2:T(8,128)S(1)}, u32[]{:S(2)}, u32[]{:S(2)}) collective-permute-start(f32[1,5,1,256]{3,1,0,2:T(8,128)S(1)} %get-tuple-element.17), channel_id=1, source_target_pairs={{1,0},{3,2},{5,4},{7,6},{9,8},{11,10},{13,12},{15,14},{17,16},{19,... | collective-permute-start | bytes 15368 | tf_op jit(solution)/shard_map/ppermute | solution.py:20
  63.9 3.8 collective-permute-start.4
  68.0 29.0 %collective-permute-start.7 = (f32[1,5,1,256]{3,1,0,2:T(8,128)S(1)}, f32[1,5,1,256]{3,1,0,2:T(8,128)S(1)}, u32[]{:S(2)}, u32[]{:S(2)}) collective-permute-start(f32[1,5,1,256]{3,1,0,2:T(8,128)S(1)} %get-tuple-element.15), channel_id=1, source_target_pairs={{1,0},{3,2},{5,4},{7,6},{9,8},{11,10},{13,12},{15,14},{17,16},{19,... | collective-permute-start | bytes 15368 | tf_op jit(solution)/shard_map/ppermute | solution.py:20
  69.3 27.7 %collective-permute-start.6 = (f32[1,5,1,256]{3,1,0,2:T(8,128)S(1)}, f32[1,5,1,256]{3,1,0,2:T(8,128)S(1)}, u32[]{:S(2)}, u32[]{:S(2)}) collective-permute-start(f32[1,5,1,256]{3,1,0,2:T(8,128)S(1)} %get-tuple-element.14), channel_id=1, source_target_pairs={{0,1},{2,3},{4,5},{6,7},{8,9},{10,11},{12,13},{14,15},{16,17},{18,... | collective-permute-start | bytes 15368 | tf_op jit(solution)/shard_map/ppermute | solution.py:19
  78.6 6.2 %copy-start.1 = (f32[2048]{0:T(1024)S(1)}, f32[2048]{0:T(1024)}, u32[]{:S(2)}) copy-start(f32[2048]{0:T(1024)} %param.16) | copy-start | bytes 24580
  98.0 16.1 %all-to-all-start = ((f32[1,5,16,256]{3,1,0,2:T(8,128)}), f32[1,5,16,256]{3,1,0,2:T(8,128)S(1)}, u32[]{:S(2)}, u32[]{:S(2)}) async-start(f32[1,5,16,256]{3,1,0,2:T(8,128)} %fusion.48), calls=%async_computation | async-start | bytes 262144 | tf_op jit(solution)/shard_map/all_to_all | solution.py:140
  106.3 128.8 %all-reduce.7.cloned.1.call-start = ((), (), s32[]{:S(2)}) async-start(), calls=%async_computation.1 | async-start | bytes 131072 | tf_op jit(solution)/shard_map/psum | solution.py:155
  118.4 118.5 %copy-start.7 = (f32[256,256]{1,0:T(8,128)S(1)}, f32[256,256]{1,0:T(8,128)}, u32[]{:S(2)}) copy-start(f32[256,256]{1,0:T(8,128)} %get-tuple-element.68) | copy-start | bytes 786436
  120.3 261.9 %all-reduce.9.cloned.1.call-start = ((), (), s32[]{:S(2)}) async-start(), calls=%async_computation.2 | async-start | bytes 1048576 | tf_op jit(solution)/shard_map/psum | solution.py:155
  236.9 2.5 copy-start.6
  239.4 2.5 copy-start.5
  241.9 2.5 copy-start.4
  386.2 1.3 copy-start.3
  387.5 1.3 copy-start.2
Sparse Core Ops, SparseCore 0:
  120.5 114.6 all-reduce.6
  253.6 128.6 all-reduce.8
where the time goes:
time: 404 us; the launch traced here: 403 us
  waiting for transfers between devices  253 us (63%)
  local copies, waits for them, and re-layouts  73.4 us (18%)
  starting transfers between devices  25.9 us (6%)
  matrix products  20.7 us (5%)
  other arithmetic  16.5 us (4%)
  between operations  14.1 us (3%)
    psum x2, waiting for transfers between devices, per_device(): priors = lax.psum(partial_priors, ('mem', 'row'))  243 us
    gather x4, local copies, waits for them, and re-layouts, per_device(): anomaly, adjust = innovations(priors, obs_value[picked], obs_var[picked])  24.6 us
    gather x2, local copies, waits for them, and re-layouts, per_device(): obs_field = field_all[picked]  12.3 us
    gather x2, local copies, waits for them, and re-layouts, per_device(): obs_row = row_all[picked]  12.3 us
    gather x2, local copies, waits for them, and re-layouts, per_device(): obs_col = col_all[picked]  12.3 us
    ppermute x4, starting transfers between devices, extended(): before = lax.ppermute(last, axis, up)  12.1 us
    dot_general x8, matrix products, regress(): lax.dot_general(centred, anomaly[:, offset:offset + obs_block], (((0,), (...  9.99 us
    dot_general x8, matrix products, regress(): lax.dot_general(adjust[:, offset:offset + obs_block], weights.reshape(n_c...  9.76 us
  transfers between devices with their start and end apart: 11, of which 5 were waited for; matrix products, arithmetic and copies ran while one was open for 17% of the time, Pallas kernels for 0%

commit v1 on v0

--- a/solution.py
+++ b/solution.py
@@ -152,7 +152,8 @@
             + obs_col
         )
         partial_priors = jnp.take(ensemble_now, local_ids, axis=1) * owned[None, :]
-        priors = lax.psum(partial_priors, ("mem", "row"))
+        one_axis = lax.psum(partial_priors, "row")
+        priors = lax.psum(one_axis, "mem")
         anomaly, adjust = innovations(priors, obs_value[picked], obs_var[picked])
         ensemble_now = regress(
             ensemble_now, base_row, obs_field, obs_row, obs_col, anomaly, adjust, field_mask, n_cols

time: 404 us -> 407 us (level)
    psum x2 -> x4, waiting for transfers between devices: 243 us -> 241 us  [the longest x2 223 us: per_device(): priors = lax.psum(one_axis, 'mem')]
  transfers between devices with their start and end apart: 11 -> 13, of which waited for: 5 -> 7; matrix products, arithmetic and copies ran while one was open for 17% -> 18% of each run, Pallas kernels for 0% -> 0%
where the time goes in v1:
time: 407 us; the launch traced here: 406 us
  waiting for transfers between devices  251 us (62%)
  local copies, waits for them, and re-layouts  73.2 us (18%)
  starting transfers between devices  26.2 us (6%)
  matrix products  24.1 us (6%)
  other arithmetic  17.9 us (4%)
  between operations  13.8 us (3%)
    psum x2, waiting for transfers between devices, per_device(): priors = lax.psum(one_axis, 'mem')  223 us
    gather x4, local copies, waits for them, and re-layouts, per_device(): anomaly, adjust = innovations(priors, obs_value[picked], obs_var[picked])  24.6 us
    psum x2, waiting for transfers between devices, per_device(): one_axis = lax.psum(partial_priors, 'row')  18.5 us
    gather x2, local copies, waits for them, and re-layouts, per_device(): obs_field = field_all[picked]  12.3 us
    gather x2, local copies, waits for them, and re-layouts, per_device(): obs_row = row_all[picked]  12.3 us
    gather x2, local copies, waits for them, and re-layouts, per_device(): obs_col = col_all[picked]  12.3 us
    ppermute x4, starting transfers between devices, extended(): before = lax.ppermute(last, axis, up)  12.1 us
    dot_general x8, matrix products, regress(): lax.dot_general(centred, anomaly[:, offset:offset + obs_block], (((0,), (...  11 us
  transfers between devices with their start and end apart: 13, of which 7 were waited for; matrix products, arithmetic and copies ran while one was open for 18% of the time, Pallas kernels for 0%

profile of v1, /device:TPU:0, one launch (start us, length us, event | category | flops | bytes accessed | tf_op | source)
XLA Modules:
  0.0 405.8 jit_solution(16601850915948569768)
XLA Ops:
  6.5 1.0 copy.33
  7.5 1.3 collective-permute-start.1
  8.8 3.0 collective-permute-start
  11.9 0.7 add_select_fusion.1
  12.6 0.7 fusion.124
  13.3 6.1 %gather_fusion.8 = s32[1024]{0:T(1024)S(1)} fusion(s32[2048]{0:T(1024)S(1)} %get-tuple-element.33, s32[1024]{0:T(1024)S(1)} %get-tuple-element.28), kind=kCustom, calls=%fused_computation.10 | custom fusion | bytes 12288 | tf_op jit(solution)/shard_map/gather | solution.py:147
  19.4 6.2 %gather_fusion.7 = s32[1024]{0:T(1024)S(1)} fusion(s32[2048]{0:T(1024)S(1)} %get-tuple-element.32, s32[1024]{0:T(1024)S(1)} %get-tuple-element.28), kind=kCustom, calls=%fused_computation.9 | custom fusion | bytes 12288 | tf_op jit(solution)/shard_map/gather | solution.py:146
  25.6 6.2 %gather_fusion.3 = s32[1024]{0:T(1024)S(1)} fusion(s32[2048]{0:T(1024)S(1)} %get-tuple-element.33, s32[1024]{0:T(1024)S(1)} %get-tuple-element.29), kind=kCustom, calls=%fused_computation.5 | custom fusion | bytes 12288 | tf_op jit(solution)/shard_map/gather | solution.py:147
  31.8 6.2 %gather_fusion.2 = s32[1024]{0:T(1024)S(1)} fusion(s32[2048]{0:T(1024)S(1)} %get-tuple-element.32, s32[1024]{0:T(1024)S(1)} %get-tuple-element.29), kind=kCustom, calls=%fused_computation.4 | custom fusion | bytes 12288 | tf_op jit(solution)/shard_map/gather | solution.py:146
  37.9 6.2 %gather_fusion.1 = s32[1024]{0:T(1024)S(1)} fusion(s32[2048]{0:T(1024)S(1)} %get-tuple-element.34, s32[1024]{0:T(1024)S(1)} %get-tuple-element.29), kind=kCustom, calls=%fused_computation.3 | custom fusion | bytes 12288 | tf_op jit(solution)/shard_map/gather | solution.py:145
  44.1 6.2 %gather_fusion.6 = s32[1024]{0:T(1024)S(1)} fusion(s32[2048]{0:T(1024)S(1)} %get-tuple-element.34, s32[1024]{0:T(1024)S(1)} %get-tuple-element.28), kind=kCustom, calls=%fused_computation.8 | custom fusion | bytes 12288 | tf_op jit(solution)/shard_map/gather | solution.py:145
  50.4 0.6 compare_and_fusion
  51.0 0.7 convolution_bitcast_fusion.7
  51.7 0.7 convolution_bitcast_fusion.6
  52.4 0.7 convolution_bitcast_fusion.5
  53.4 3.8 fusion.25
  57.5 0.7 convolution_bitcast_fusion.4
  58.5 1.3 collective-permute-start.3
  59.8 3.0 collective-permute-start.2
  62.9 0.7 collective-permute-done.2
  63.9 1.3 collective-permute-start.5
  65.2 3.0 collective-permute-start.4
  68.4 0.7 collective-permute-done.4
  69.3 1.3 collective-permute-start.7
  70.6 3.0 collective-permute-start.6
  73.7 6.2 %gather_fusion = f32[1024]{0:T(1024)S(1)} fusion(f32[2048]{0:T(1024)S(1)} %copy-done, s32[1024]{0:T(1024)S(1)} %get-tuple-element.29), kind=kCustom, calls=%fused_computation.2 | custom fusion | bytes 12288 | tf_op jit(solution)/shard_map/gather | solution.py:157
  79.9 6.2 %gather_fusion.4 = f32[1024]{0:T(1024)S(1)} fusion(f32[2048]{0:T(1024)S(1)} %copy-done.1, s32[1024]{0:T(1024)S(1)} %get-tuple-element.29), kind=kCustom, calls=%fused_computation.6 | custom fusion | bytes 12288 | tf_op jit(solution)/shard_map/gather | solution.py:157
  86.2 0.8 fusion.48
  87.0 8.3 %all-to-all-start = ((f32[1,5,16,256]{3,1,0,2:T(8,128)}), f32[1,5,16,256]{3,1,0,2:T(8,128)S(1)}, u32[]{:S(2)}, u32[]{:S(2)}) async-start(f32[1,5,16,256]{3,1,0,2:T(8,128)} %fusion.48), calls=%async_computation | async-start | bytes 262144 | tf_op jit(solution)/shard_map/all_to_all | solution.py:140
  95.4 7.7 %all-to-all-done = f32[1,5,16,256]{3,1,0,2:T(8,128)S(1)} async-done(((f32[1,5,16,256]{3,1,0,2:T(8,128)}), f32[1,5,16,256]{3,1,0,2:T(8,128)S(1)}, u32[]{:S(2)}, u32[]{:S(2)}) %all-to-all-start) | async-done | bytes 81952 | tf_op jit(solution)/shard_map/all_to_all | solution.py:140
  103.4 4.0 gather_fusion.10
  107.4 1.2 copy.39
  108.6 1.3 bitcast_multiply_fusion.1
  110.0 15.0 %all-reduce.9.cloned.1.call-done = f32[16,1024]{1,0:T(8,128)} async-done(((f32[16,1024]{1,0:T(8,128)}), f32[16,1024]{1,0:T(8,128)}) %all-reduce.9.cloned.1.call-update) | async-done | bytes 65552 | tf_op jit(solution)/shard_map/psum | solution.py:155
  125.3 108.4 %all-reduce.11.cloned.1.call-done = f32[16,1024]{1,0:T(8,128)} async-done(((f32[16,1024]{1,0:T(8,128)}), f32[16,1024]{1,0:T(8,128)}) %all-reduce.11.cloned.1.call-update) | async-done | bytes 65552 | tf_op jit(solution)/shard_map/psum | solution.py:156
  233.6 0.9 reduce_sum.54
  234.5 0.9 multiply_reduce_fusion.1
  235.4 2.2 fusion.9
  237.7 1.2 fusion.115
  238.9 1.3 fusion.8
  240.2 1.2 convolution_add_fusion.5
  241.4 1.2 fusion.7
  242.7 1.2 convolution_add_fusion.4
  243.9 1.3 fusion.6
  245.1 1.2 fusion.152
  246.6 4.0 gather_fusion.11
  250.6 2.2 bitcast_multiply_fusion
  253.2 1.8 broadcast_multiply_fusion
  255.0 6.1 %gather_fusion.5 = f32[1024]{0:T(1024)S(1)} fusion(f32[2048]{0:T(1024)S(1)} %copy-done, s32[1024]{0:T(1024)S(1)} %get-tuple-element.28), kind=kCustom, calls=%fused_computation.7 | custom fusion | bytes 12288 | tf_op jit(solution)/shard_map/gather | solution.py:157
  261.1 6.2 %gather_fusion.9 = f32[1024]{0:T(1024)S(1)} fusion(f32[2048]{0:T(1024)S(1)} %copy-done.1, s32[1024]{0:T(1024)S(1)} %get-tuple-element.28), kind=kCustom, calls=%fused_computation.11 | custom fusion | bytes 12288 | tf_op jit(solution)/shard_map/gather | solution.py:157
  267.3 3.6 all-reduce.13.cloned.1.call-done
  270.9 114.5 %all-reduce.15.cloned.1.call-done = f32[16,1024]{0,1:T(8,128)} async-done(((f32[16,1024]{0,1:T(8,128)}), f32[16,1024]{0,1:T(8,128)}) %all-reduce.15.cloned.1.call-update) | async-done | bytes 65552 | tf_op jit(solution)/shard_map/psum | solution.py:156
  385.4 1.2 reduce_sum.57
  386.6 1.4 multiply_reduce_fusion
  388.0 1.3 fusion
  389.3 1.2 fusion.1
  390.6 1.2 fusion.2
  391.9 1.2 fusion.3
  393.2 0.3 multiply_subtract_fusion
  393.6 1.2 fusion.42
  394.8 1.3 convolution_add_fusion.2
  396.1 1.3 convolution_add_fusion.1
  397.3 1.3 fusion.4
  398.6 0.7 reshape.1048
  (86 shorter events, 3.1 us)
Async XLA Ops:
  6.5 67.1 %copy-start = (f32[2048]{0:T(1024)S(1)}, f32[2048]{0:T(1024)}, u32[]{:S(2)}) copy-start(f32[2048]{0:T(1024)} %param.15) | copy-start | bytes 24580
  7.5 50.7 %collective-permute-start.1 = (f32[1,5,1,256]{3,1,0,2:T(8,128)S(1)}, f32[1,5,1,256]{3,1,0,2:T(8,128)S(1)}, u32[]{:S(2)}, u32[]{:S(2)}) collective-permute-start(f32[1,5,1,256]{3,1,0,2:T(8,128)S(1)} %get-tuple-element.21), channel_id=1, source_target_pairs={{1,0},{3,2},{5,4},{7,6},{9,8},{11,10},{13,12},{15,14},{17,16},{19,... | collective-permute-start | bytes 15368 | tf_op jit(solution)/shard_map/ppermute | solution.py:20
  8.8 49.4 %collective-permute-start = (f32[1,5,1,256]{3,1,0,2:T(8,128)S(1)}, f32[1,5,1,256]{3,1,0,2:T(8,128)S(1)}, u32[]{:S(2)}, u32[]{:S(2)}) collective-permute-start(f32[1,5,1,256]{3,1,0,2:T(8,128)S(1)} %get-tuple-element.20), channel_id=1, source_target_pairs={{0,1},{2,3},{4,5},{6,7},{8,9},{10,11},{12,13},{14,15},{16,17},{18,... | collective-permute-start | bytes 15368 | tf_op jit(solution)/shard_map/ppermute | solution.py:19
  44.1 6.2 %copy-start.10 = (f32[2,16,256]{2,1,0:T(8,128)S(1)}, f32[2,16,256]{2,1,0:T(8,128)}, u32[]{:S(2)}) copy-start(f32[2,16,256]{2,1,0:T(8,128)} %param.11) | copy-start | bytes 98308
  44.1 6.9 %copy-start.9 = (s32[5,5]{1,0:T(8,128)S(1)}, s32[5,5]{1,0:T(8,128)}, u32[]{:S(2)}) copy-start(s32[5,5]{1,0:T(8,128)} %param.17) | copy-start | bytes 304
  57.2 1.1 copy-start.15
  58.5 4.5 %collective-permute-start.3 = (f32[1,5,1,256]{3,1,0,2:T(8,128)S(1)}, f32[1,5,1,256]{3,1,0,2:T(8,128)S(1)}, u32[]{:S(2)}, u32[]{:S(2)}) collective-permute-start(f32[1,5,1,256]{3,1,0,2:T(8,128)S(1)} %get-tuple-element.19), channel_id=1, source_target_pairs={{1,0},{3,2},{5,4},{7,6},{9,8},{11,10},{13,12},{15,14},{17,16},{19,... | collective-permute-start | bytes 15368 | tf_op jit(solution)/shard_map/ppermute | solution.py:20
  59.8 3.8 collective-permute-start.2
  63.9 4.5 %collective-permute-start.5 = (f32[1,5,1,256]{3,1,0,2:T(8,128)S(1)}, f32[1,5,1,256]{3,1,0,2:T(8,128)S(1)}, u32[]{:S(2)}, u32[]{:S(2)}) collective-permute-start(f32[1,5,1,256]{3,1,0,2:T(8,128)S(1)} %get-tuple-element.17), channel_id=1, source_target_pairs={{1,0},{3,2},{5,4},{7,6},{9,8},{11,10},{13,12},{15,14},{17,16},{19,... | collective-permute-start | bytes 15368 | tf_op jit(solution)/shard_map/ppermute | solution.py:20
  65.2 3.8 collective-permute-start.4
  69.3 16.7 %collective-permute-start.7 = (f32[1,5,1,256]{3,1,0,2:T(8,128)S(1)}, f32[1,5,1,256]{3,1,0,2:T(8,128)S(1)}, u32[]{:S(2)}, u32[]{:S(2)}) collective-permute-start(f32[1,5,1,256]{3,1,0,2:T(8,128)S(1)} %get-tuple-element.15), channel_id=1, source_target_pairs={{1,0},{3,2},{5,4},{7,6},{9,8},{11,10},{13,12},{15,14},{17,16},{19,... | collective-permute-start | bytes 15368 | tf_op jit(solution)/shard_map/ppermute | solution.py:20
  70.6 15.4 %collective-permute-start.6 = (f32[1,5,1,256]{3,1,0,2:T(8,128)S(1)}, f32[1,5,1,256]{3,1,0,2:T(8,128)S(1)}, u32[]{:S(2)}, u32[]{:S(2)}) collective-permute-start(f32[1,5,1,256]{3,1,0,2:T(8,128)S(1)} %get-tuple-element.14), channel_id=1, source_target_pairs={{0,1},{2,3},{4,5},{6,7},{8,9},{10,11},{12,13},{14,15},{16,17},{18,... | collective-permute-start | bytes 15368 | tf_op jit(solution)/shard_map/ppermute | solution.py:19
  73.7 6.2 %copy-start.1 = (f32[2048]{0:T(1024)S(1)}, f32[2048]{0:T(1024)}, u32[]{:S(2)}) copy-start(f32[2048]{0:T(1024)} %param.16) | copy-start | bytes 24580
  87.0 16.1 %all-to-all-start = ((f32[1,5,16,256]{3,1,0,2:T(8,128)}), f32[1,5,16,256]{3,1,0,2:T(8,128)S(1)}, u32[]{:S(2)}, u32[]{:S(2)}) async-start(f32[1,5,16,256]{3,1,0,2:T(8,128)} %fusion.48), calls=%async_computation | async-start | bytes 262144 | tf_op jit(solution)/shard_map/all_to_all | solution.py:140
  95.3 29.7 %all-reduce.9.cloned.1.call-start = ((), (), s32[]{:S(2)}) async-start(), calls=%async_computation.1 | async-start | bytes 131072 | tf_op jit(solution)/shard_map/psum | solution.py:155
  107.4 128.0 %copy-start.13 = (f32[5,256]{1,0:T(8,128)S(1)}, f32[5,256]{1,0:T(8,128)}, u32[]{:S(2)}) copy-start(f32[5,256]{1,0:T(8,128)} %convolution_bitcast_fusion.7) | copy-start | bytes 15364
  109.9 123.7 %all-reduce.11.cloned.1.call-start = ((), (), s32[]{:S(2)}) async-start(), calls=%async_computation.2 | async-start | bytes 131072 | tf_op jit(solution)/shard_map/psum | solution.py:156
  125.0 145.8 %all-reduce.13.cloned.1.call-start = ((), (), s32[]{:S(2)}) async-start(), calls=%async_computation.3 | async-start | bytes 1048576 | tf_op jit(solution)/shard_map/psum | solution.py:155
  235.4 3.5 copy-start.8
  235.4 3.5 copy-start.12
  238.9 2.5 copy-start.7
  238.9 2.5 copy-start.11
  241.4 2.5 copy-start.6
  241.4 2.5 copy-start.14
  250.6 2.6 copy-start.4
  250.6 2.6 copy-start.5
  252.9 132.5 %all-reduce.15.cloned.1.call-start = ((), (), s32[]{:S(2)}) async-start(), calls=%async_computation.4 | async-start | bytes 1048576 | tf_op jit(solution)/shard_map/psum | solution.py:156
  389.3 1.3 copy-start.3
  390.6 1.3 copy-start.2
Sparse Core Ops, SparseCore 0:
  110.1 14.8 all-reduce.8
  130.5 103.1 all-reduce.10
  253.0 17.7 all-reduce.12
  275.8 109.4 all-reduce.14
